TPU v7x, 256 devices: a whole 4x4x8 slice. The times are simulated.
256 devices in a mesh: ctx: 8 (over z_hi, core), vocab: 32 (over x, y, z_lo).
Axes of the slice: x: 4, y: 4, z: 8 (z_hi: 4, z_lo: 2; z = z_hi * 2 + z_lo), core: 2. Of those that a mesh axis runs over, the one named last changes fastest.
Arguments:
- hidden: bfloat16 [512, 2, 7168], P('ctx', None, 'vocab'), may hold values from -30 to 30
- head: bfloat16 [7168, 65536], P('ctx', 'vocab'), may hold values from -0.15 to 0.15
- targets: int32 [512, 2], P('ctx'), may hold values from 0 to 65535
- loss_weight: float32 [512, 2], P('ctx'), may hold values from 16 to 256
Outputs:
- token_loss: float32 [512, 2], P('ctx')
- grad_hidden: bfloat16 [512, 2, 7168], P('ctx', None, 'vocab')
All inputs are finite; a program needn't handle non-finite values.
Results may differ from a plain program's by a relative error of at most 0.0046.
Values may be sent and summed in bfloat16 or wider, within the bound.
A program may use at most 64 MiB of HBM per device.

v0:
```python
import jax
import jax.numpy as jnp
from jax import lax
from jax.sharding import PartitionSpec as P


def sent_to_all(x, axis):
    copies = jnp.broadcast_to(x, (lax.axis_size(axis), *x.shape))
    return lax.all_to_all(copies, axis, split_axis=0, concat_axis=0, tiled=True)


def gathered_once(x, axis):
    leaves = jax.tree.leaves(x)
    order = sorted(range(len(leaves)), key=lambda k: -leaves[k].size)
    width = (1, *leaves[order[0]].shape)[-1]
    lines = [
        jnp.pad(leaves[k].reshape(-1), (0, -leaves[k].size % width)).reshape(-1, width)
        for k in order
    ]
    both, at, found = (sent_to_all(jnp.concatenate(lines), axis), 0, {})
    for k, line in zip(order, lines):
        slab = both[:, at : at + len(line)].reshape(len(both), -1)
        found[k] = slab[:, : leaves[k].size].reshape(-1, *leaves[k].shape)
        at += len(line)
    numbers = iter(range(len(leaves)))
    return jax.tree.map(lambda _: found[next(numbers)], x)


def combined_pairwise(pieces, combine):
    while len(jax.tree.leaves(pieces)[0]) > 1:
        pieces = jax.vmap(combine)(
            *(jax.tree.map(lambda part: part[side::2], pieces) for side in (0, 1))
        )
    return jax.tree.map(lambda part: part[0], pieces)


def joined_all(x, axis, combine):
    pieces = gathered_once(x, axis)
    return combined_pairwise(pieces, combine)


def cut_along(x, dim, size):
    lengths = x.shape
    pieces = x.reshape(*lengths[:dim], size, lengths[dim] // size, *lengths[dim + 1 :])
    return jnp.moveaxis(pieces, dim, 0)


def summed_on_arrival(x, axis, dim):
    pieces = cut_along(x, dim, lax.axis_size(axis))
    arrived = lax.all_to_all(pieces, axis, split_axis=0, concat_axis=0, tiled=True)
    return arrived.sum(axis=0)


def combine_stats(first, second):
    first_max, first_sum, first_target = first
    second_max, second_sum, second_target = second
    joined = jnp.maximum(first_max, second_max)
    total = first_sum * jnp.exp(first_max - joined) + second_sum * jnp.exp(second_max - joined)
    return (joined, total, first_target + second_target)


def body(hidden, head, targets, loss_weight):
    group_rows = hidden.shape[0]
    depth_count = hidden.shape[1]
    flat_count = group_rows * depth_count
    ctx_count = lax.axis_size("ctx")
    vocab_count = lax.axis_size("vocab")
    vocab_index = lax.axis_index("vocab")
    vocab_local = head.shape[1]
    flat_hidden = hidden.reshape(flat_count, hidden.shape[2])
    flat_targets = targets.reshape(flat_count)
    flat_weights = loss_weight.reshape(flat_count)
    whole_width = lax.all_gather(flat_hidden, "vocab", axis=1, tiled=True)
    width_slab = lax.all_to_all(whole_width, "ctx", split_axis=1, concat_axis=0, tiled=True)
    logits = lax.psum_scatter(
        jnp.dot(width_slab, head, preferred_element_type=jnp.float32),
        "ctx",
        scatter_dimension=0,
        tiled=True,
    )
    columns = vocab_index * vocab_local + lax.broadcasted_iota(jnp.int32, logits.shape, 1)
    target_hit = columns == flat_targets[:, None]
    local_max = jnp.max(logits, axis=1)
    local_target = jnp.sum(jnp.where(target_hit, logits, 0.0), axis=1)
    local_sum = jnp.sum(jnp.exp(logits - local_max[:, None]), axis=1)
    row_max, sum_exp, target_logit = joined_all(
        (local_max, local_sum, local_target), "vocab", combine_stats
    )
    flat_loss = jnp.log(sum_exp) + row_max - target_logit
    token_loss = flat_loss.reshape(group_rows, depth_count)
    probabilities = jnp.exp(logits - row_max[:, None]) / sum_exp[:, None]
    dlogits = (flat_weights[:, None] * (probabilities - target_hit.astype(jnp.float32))).astype(
        jnp.bfloat16
    )
    grad_slab = lax.dot_general(
        lax.all_gather(dlogits, "ctx", axis=0, tiled=True),
        head,
        (((1,), (1,)), ((), ())),
        preferred_element_type=jnp.float32,
    )
    share_rows = flat_count // vocab_count
    slab_width = grad_slab.shape[1]
    blocks = grad_slab.reshape(ctx_count, vocab_count, share_rows, slab_width)
    reduced = summed_on_arrival(blocks, "vocab", 1).astype(jnp.bfloat16)
    landed = lax.all_to_all(
        lax.all_to_all(reduced, "ctx", split_axis=0, concat_axis=3, tiled=True),
        "vocab",
        split_axis=3,
        concat_axis=1,
        tiled=True,
    )
    grad_out = landed.reshape(group_rows, depth_count, landed.shape[3])
    return (token_loss, grad_out)


def solution(mesh):
    return jax.shard_map(
        body,
        mesh=mesh,
        in_specs=(P("ctx", None, "vocab"), P("ctx", "vocab"), P("ctx", None), P("ctx", None)),
        out_specs=(P("ctx", None), P("ctx", None, "vocab")),
        check_vma=False,
    )
```

profile of v0, /device:TPU:1, one launch (start us, length us, event | category | flops | bytes accessed | tf_op | source)
XLA Modules:
  0.0 565.0 jit_solution(5996300982655620662)
XLA Ops:
  7.2 0.0 all-gather.3.cloned.1.call-start
  7.2 0.9 reshape.54
  8.1 0.7 copy.29
  8.8 0.0 all-gather.3.cloned.1.call-update
  8.9 0.0 reduce-scatter.2.cloned.1.call-start
  8.9 141.3 %all-gather.3.cloned.1.call-done = bf16[128,7168]{0,1:T(8,128)(2,1)} async-done(((bf16[128,224]{0,1:T(8,128)(2,1)}), bf16[128,7168]{0,1:T(8,128)(2,1)}) %all-gather.3.cloned.1.call-update) | async-done | bytes 1835024 | tf_op jit(solution)/shard_map/all_gather | solution.py:73
  150.2 72.8 %all_to_all.62 = bf16[128,8,896]{0,2,1:T(8,128)(2,1)S(1)} all-to-all(bf16[128,8,896]{0,2,1:T(8,128)(2,1)} %bitcast.42), channel_id=1, replica_groups=mesh['ctx'=8,'vocab'=32] {'ctx'}, dimensions={1} | all-to-all | bytes 3670016 | tf_op jit(solution)/shard_map/all_to_all | solution.py:74
  222.9 2.7 copy.30
  225.6 10.3 %fusion.6 = f32[1024,2048]{1,0:T(8,128)} fusion(bf16[1024,896]{1,0:T(8,128)(2,1)} %bitcast.43, bf16[896,2048]{1,0:T(8,128)(2,1)} %param.5), kind=kOutput, calls=%fused_computation.20 | convolution fusion | flops 3758096384 | bytes 13893632 | tf_op jit(solution)/shard_map/dot_general | solution.py:76
  235.9 0.0 copy-start
  236.0 0.0 copy-start.1
  236.0 0.0 reduce-scatter.2.cloned.1.call-update
  236.0 0.6 copy-done
  236.6 0.1 copy.31
  236.7 0.1 eq.10
  236.9 88.8 %reduce-scatter.2.cloned.1.call-done = f32[128,2048]{1,0:T(8,128)} async-done(((f32[1024,2048]{1,0:T(8,128)}), f32[128,2048]{1,0:T(8,128)}) %reduce-scatter.2.cloned.1.call-update) | async-done | bytes 1048592 | tf_op jit(solution)/shard_map/reduce_scatter | solution.py:75
  325.7 1.4 reduce_max.9
  327.0 1.6 exponential_reduce_fusion
  328.6 0.6 broadcast_in_dim.9
  329.3 8.1 %all-to-all-start.1 = ((f32[32,3,128]{2,1,0:T(4,128)}), f32[32,3,128]{2,1,0:T(4,128)S(1)}, u32[]{:S(2)}, u32[]{:S(2)}) async-start(f32[32,3,128]{2,1,0:T(4,128)} %broadcast_in_dim.9), calls=%async_computation.2 | async-start | bytes 131072 | tf_op jit(solution)/shard_map/all_to_all | solution.py:9
  337.4 0.0 all-gather.5.cloned.1.call-start
  337.5 0.0 copy-done.1
  337.5 0.1 copy.34
  337.6 0.1 mul.54
  337.7 6.9 %all-to-all-done.1 = f32[32,3,128]{2,1,0:T(4,128)S(1)} async-done(((f32[32,3,128]{2,1,0:T(4,128)}), f32[32,3,128]{2,1,0:T(4,128)S(1)}, u32[]{:S(2)}, u32[]{:S(2)}) %all-to-all-start.1) | async-done | bytes 49184 | tf_op jit(solution)/shard_map/all_to_all | solution.py:9
  345.2 2.4 fusion.3
  347.6 0.0 all-gather.5.cloned.1.call-update
  347.7 51.8 %all-gather.5.cloned.1.call-done = bf16[1024,2048]{1,0:T(8,128)(2,1)} async-done(((bf16[128,2048]{1,0:T(8,128)(2,1)}), bf16[1024,2048]{1,0:T(8,128)(2,1)}) %all-gather.5.cloned.1.call-update) | async-done | bytes 4194320 | tf_op jit(solution)/shard_map/all_gather | solution.py:96
  399.5 9.7 %fusion.7 = f32[1024,896]{1,0:T(8,128)} fusion(bf16[1024,2048]{1,0:T(8,128)(2,1)} %all-gather.5.cloned.1.call-done, bf16[896,2048]{1,0:T(8,128)(2,1)} %param.5), kind=kOutput, calls=%fused_computation.21 | convolution fusion | flops 3758096384 | bytes 11534336 | tf_op jit(solution)/shard_map/dot_general | solution.py:95
  409.2 5.0 reshape_reshape.3
  414.2 3.1 copy.46
  417.2 52.6 %all_to_all.63 = f32[32,8,1,4,896]{4,3,1,2,0:T(4,128)} all-to-all(f32[32,8,1,4,896]{4,3,1,2,0:T(4,128)S(1)} %bitcast.38), channel_id=1, replica_groups=mesh['ctx'=8,'vocab'=32] {'vocab'}, dimensions={0} | all-to-all | bytes 7340032 | tf_op jit(solution)/shard_map/all_to_all | solution.py:50
  469.9 2.7 reduce_sum.29
  472.5 12.3 %all_to_all.64 = bf16[8,1,4,896]{3,2,1,0:T(4,128)(2,1)S(1)} all-to-all(bf16[8,1,4,896]{3,2,1,0:T(4,128)(2,1)S(1)} %bitcast.45), channel_id=1, replica_groups=mesh['ctx'=8,'vocab'=32] {'ctx'}, dimensions={0} | all-to-all | bytes 114688 | tf_op jit(solution)/shard_map/all_to_all | solution.py:106
  484.8 6.0 %copy.38 = bf16[1,1,4,7168]{2,1,0,3:T(2,128)(2,1)} copy(bf16[1,1,4,7168]{3,2,1,0:T(4,128)(2,1)S(1)} %bitcast.46) | data formatting | bytes 114688 | tf_op jit(solution)/shard_map/all_to_all | solution.py:106
  490.8 0.5 broadcast.6
  491.3 39.8 %reduce.5 = bf16[7168,4]{1,0:T(8,128)(2,1)S(1)} reduce(bf16[7168,1,1,4]{3,2,1,0:T(2,128)(2,1)} %bitcast.40, bf16[]{:T(256)} %broadcast.6), dimensions={1,2}, to_apply=%bitcast.31.reduce_sub_computation | reduce | bytes 114690
  531.1 2.5 reshape.69
  533.6 3.9 all-to-all-start.4
  537.5 0.1 sub.71
  537.6 0.6 copy.41
  538.2 6.5 %all-to-all-done.4 = bf16[32,2,448]{2,1,0:T(2,128)(2,1)S(1)} async-done(((bf16[32,2,448]{2,1,0:T(2,128)(2,1)}), bf16[32,2,448]{2,1,0:T(2,128)(2,1)S(1)}, u32[]{:S(2)}, u32[]{:S(2)}) %all-to-all-start.4) | async-done | bytes 57376 | tf_op jit(solution)/shard_map/all_to_all | solution.py:105
  544.7 5.7 %reshape.70 = bf16[7168,1,1,4]{3,2,1,0:T(2,128)(2,1)} reshape(bf16[32,2,448]{2,1,0:T(2,128)(2,1)S(1)} %all-to-all-done.4) | data formatting | bytes 114688
  550.5 7.1 %copy.39 = bf16[1,1,4,7168]{3,2,1,0:T(4,128)(2,1)S(1)} copy(bf16[1,1,4,7168]{2,1,0,3:T(2,128)(2,1)} %bitcast.39) | data formatting | bytes 114688 | tf_op jit(solution)/shard_map/all_to_all | solution.py:105
  557.6 0.1 all_to_all.55
  557.7 0.1 copy.40
  557.8 0.7 reshape.61
  (36 shorter events, 0.5 us)
Async XLA Ops:
  7.2 143.0 %all-gather.3.cloned.1.call-start = ((), (), s32[]{:S(2)}) async-start(), calls=%async_computation.6 | async-start | bytes 1892352 | tf_op jit(solution)/shard_map/all_gather | solution.py:73
  8.9 316.8 %reduce-scatter.2.cloned.1.call-start = ((), (), s32[]{:S(2)}) async-start(), calls=%async_computation.7 | async-start | bytes 9437184 | tf_op jit(solution)/shard_map/reduce_scatter | solution.py:75
  235.9 0.7 copy-start
  236.0 101.5 %copy-start.1 = (f32[64,2]{0,1:T(2,128)S(1)}, f32[64,2]{0,1:T(2,128)}, u32[]{:S(2)}) copy-start(f32[64,2]{0,1:T(2,128)} %param.7) | copy-start | bytes 1540
  329.3 15.3 %all-to-all-start.1 = ((f32[32,3,128]{2,1,0:T(4,128)}), f32[32,3,128]{2,1,0:T(4,128)S(1)}, u32[]{:S(2)}, u32[]{:S(2)}) async-start(f32[32,3,128]{2,1,0:T(4,128)} %broadcast_in_dim.9), calls=%async_computation.2 | async-start | bytes 131072 | tf_op jit(solution)/shard_map/all_to_all | solution.py:9
  337.4 62.1 %all-gather.5.cloned.1.call-start = ((), (), s32[]{:S(2)}) async-start(), calls=%async_computation.8 | async-start | bytes 4718592 | tf_op jit(solution)/shard_map/all_gather | solution.py:96
  533.6 11.1 %all-to-all-start.4 = ((bf16[32,2,448]{2,1,0:T(2,128)(2,1)}), bf16[32,2,448]{2,1,0:T(2,128)(2,1)S(1)}, u32[]{:S(2)}, u32[]{:S(2)}) async-start(bf16[32,2,448]{2,1,0:T(2,128)(2,1)} %reshape.69), calls=%async_computation.5 | async-start | bytes 131072 | tf_op jit(solution)/shard_map/all_to_all | solution.py:105
Sparse Core Ops, SparseCore 0:
  10.3 139.7 all-gather.2
  236.1 89.5 reduce-scatter.1
  347.8 51.6 all-gather.4
where the time goes:
time: 566 us; the launch traced here: 565 us
  waiting for transfers between devices  295 us (52%)
  blocking collectives  138 us (24%)
  other arithmetic  47.9 us (8%)
  local copies, waits for them, and re-layouts  38.1 us (7%)
  matrix products  20 us (4%)
  between operations  13.9 us (2%)
  starting transfers between devices  12.1 us (2%)
    all_gather x1, waiting for transfers between devices, body(): whole_width = lax.all_gather(flat_hidden, 'vocab', axis=1, tiled=True)  141 us
    reduce_scatter x1, waiting for transfers between devices, body(): lax.psum_scatter(jnp.dot(width_slab, head, preferred_element_type=jnp.flo...  88.8 us
    all_to_all x1, blocking collectives, body(): lax.all_to_all(whole_width, 'ctx', split_axis=1, concat_axis=0, tiled=True)  72.8 us
    all_to_all x1, blocking collectives, summed_on_arrival(): lax.all_to_all(pieces, axis, split_axis=0, concat_axis=0, tiled=True)  52.6 us
    all_gather x1, waiting for transfers between devices, body(): lax.all_gather(dlogits, 'ctx', axis=0, tiled=True)  51.8 us
    unnamed x1, other arithmetic  39.8 us
    all_to_all x1, blocking collectives, body(): lax.all_to_all(reduced, 'ctx', split_axis=0, concat_axis=3, tiled=True)  12.3 us
  transfers between devices with their start and end apart: 5, of which 5 were waited for; matrix products, arithmetic and copies ran while one was open for 0% of the time, Pallas kernels for 0%

commit v1 on v0

--- a/solution.py
+++ b/solution.py
@@ -2,6 +2,12 @@
 import jax.numpy as jnp
 from jax import lax
 from jax.sharding import PartitionSpec as P
+from jax.lax import all_to_all, psum
+
+
+def report_vectors(mine):
+    y2 = jnp.stack(jnp.split(mine, psum(1, "vocab"), 3), 0)
+    return jnp.concatenate(all_to_all(y2, axis_name="vocab", split_axis=0, concat_axis=0), 1)
 
 
 def sent_to_all(x, axis):
@@ -102,13 +108,7 @@
     slab_width = grad_slab.shape[1]
     blocks = grad_slab.reshape(ctx_count, vocab_count, share_rows, slab_width)
     reduced = summed_on_arrival(blocks, "vocab", 1).astype(jnp.bfloat16)
-    landed = lax.all_to_all(
-        lax.all_to_all(reduced, "ctx", split_axis=0, concat_axis=3, tiled=True),
-        "vocab",
-        split_axis=3,
-        concat_axis=1,
-        tiled=True,
-    )
+    landed = report_vectors(lax.all_to_all(reduced, "ctx", split_axis=0, concat_axis=3, tiled=True))
     grad_out = landed.reshape(group_rows, depth_count, landed.shape[3])
     return (token_loss, grad_out)
 

time: 566 us -> 524 us (0.926)
  other arithmetic: 47.9 us -> 8.19 us
    unnamed x1 -> x0, other arithmetic: 39.8 us -> none
    all_to_all x4 -> x0, local copies, waits for them, and re-layouts: 13.3 us -> none  [the longest x3 7.3 us: body(): lax.all_to_all(lax.all_to_all(reduced, 'ctx', split_axis=0, concat_axis=3...]
    unnamed x10 -> x38, local copies, waits for them, and re-layouts: 10.2 us -> 21.1 us
where the time goes in v1:
time: 524 us
  waiting for transfers between devices  295 us (56%)
  blocking collectives  138 us (26%)
  local copies, waits for them, and re-layouts  36.3 us (7%)
  matrix products  20 us (4%)
  between operations  13.9 us (3%)
  starting transfers between devices  12.2 us (2%)
  other arithmetic  8.19 us (2%)
    all_gather x1, waiting for transfers between devices, body(): whole_width = lax.all_gather(flat_hidden, 'vocab', axis=1, tiled=True)  141 us
    reduce_scatter x1, waiting for transfers between devices, body(): lax.psum_scatter(jnp.dot(width_slab, head, preferred_element_type=jnp.flo...  88.6 us
    all_to_all x1, blocking collectives, body(): lax.all_to_all(whole_width, 'ctx', split_axis=1, concat_axis=0, tiled=True)  72.8 us
    all_to_all x1, blocking collectives, summed_on_arrival(): lax.all_to_all(pieces, axis, split_axis=0, concat_axis=0, tiled=True)  52.6 us
    all_gather x1, waiting for transfers between devices, body(): lax.all_gather(dlogits, 'ctx', axis=0, tiled=True)  51.9 us
    unnamed x38, local copies, waits for them, and re-layouts  21.1 us
    all_to_all x1, blocking collectives, body(): lax.all_to_all(reduced, 'ctx', split_axis=0, concat_axis=3, tiled=True)  12.3 us
  transfers between devices with their start and end apart: 5, of which 5 were waited for; matrix products, arithmetic and copies ran while one was open for 0% of the time, Pallas kernels for 0%

profile of v1, /device:TPU:1, one launch (start us, length us, event | category | flops | bytes accessed | tf_op | source)
XLA Modules:
  0.0 523.6 jit_solution(2961222836083256144)
XLA Ops:
  7.2 0.9 reshape.50
  8.1 0.7 copy.84
  8.9 0.0 reduce-scatter.2.cloned.1.call-start
  8.9 141.3 %all-gather.3.cloned.1.call-done = bf16[128,7168]{0,1:T(8,128)(2,1)} async-done(((bf16[128,224]{0,1:T(8,128)(2,1)}), bf16[128,7168]{0,1:T(8,128)(2,1)}) %all-gather.3.cloned.1.call-update) | async-done | bytes 1835024 | tf_op jit(solution)/shard_map/all_gather | solution.py:79
  150.2 72.8 %all_to_all.52 = bf16[128,8,896]{0,2,1:T(8,128)(2,1)S(1)} all-to-all(bf16[128,8,896]{0,2,1:T(8,128)(2,1)} %bitcast.163), channel_id=1, replica_groups=mesh['ctx'=8,'vocab'=32] {'ctx'}, dimensions={1} | all-to-all | bytes 3670016 | tf_op jit(solution)/shard_map/all_to_all | solution.py:80
  222.9 2.7 copy.85
  225.6 10.3 %fusion.6 = f32[1024,2048]{1,0:T(8,128)} fusion(bf16[1024,896]{1,0:T(8,128)(2,1)} %bitcast.164, bf16[896,2048]{1,0:T(8,128)(2,1)} %param.5), kind=kOutput, calls=%fused_computation.84 | convolution fusion | flops 3758096384 | bytes 13893632 | tf_op jit(solution)/shard_map/dot_general | solution.py:82
  235.9 0.6 copy-done
  236.6 0.1 copy.86
  236.7 0.1 eq.10
  236.8 88.6 %reduce-scatter.2.cloned.1.call-done = f32[128,2048]{1,0:T(8,128)} async-done(((f32[1024,2048]{1,0:T(8,128)}), f32[128,2048]{1,0:T(8,128)}) %reduce-scatter.2.cloned.1.call-update) | async-done | bytes 1048592 | tf_op jit(solution)/shard_map/reduce_scatter | solution.py:81
  325.5 1.4 reduce_max.9
  326.8 1.6 exponential_reduce_fusion
  328.5 0.6 broadcast_in_dim.9
  329.1 8.3 %all-to-all-start.1 = ((f32[32,3,128]{2,1,0:T(4,128)}), f32[32,3,128]{2,1,0:T(4,128)S(1)}, u32[]{:S(2)}, u32[]{:S(2)}) async-start(f32[32,3,128]{2,1,0:T(4,128)} %broadcast_in_dim.9), calls=%async_computation.2 | async-start | bytes 131072 | tf_op jit(solution)/shard_map/all_to_all | solution.py:15
  337.4 0.0 all-gather.5.cloned.1.call-start
  337.4 0.1 copy.89
  337.5 0.1 mul.54
  337.7 6.9 %all-to-all-done.1 = f32[32,3,128]{2,1,0:T(4,128)S(1)} async-done(((f32[32,3,128]{2,1,0:T(4,128)}), f32[32,3,128]{2,1,0:T(4,128)S(1)}, u32[]{:S(2)}, u32[]{:S(2)}) %all-to-all-start.1) | async-done | bytes 49184 | tf_op jit(solution)/shard_map/all_to_all | solution.py:15
  345.2 2.4 fusion.3
  347.6 51.9 %all-gather.5.cloned.1.call-done = bf16[1024,2048]{1,0:T(8,128)(2,1)} async-done(((bf16[128,2048]{1,0:T(8,128)(2,1)}), bf16[1024,2048]{1,0:T(8,128)(2,1)}) %all-gather.5.cloned.1.call-update) | async-done | bytes 4194320 | tf_op jit(solution)/shard_map/all_gather | solution.py:102
  399.5 9.7 %fusion.7 = f32[1024,896]{1,0:T(8,128)} fusion(bf16[1024,2048]{1,0:T(8,128)(2,1)} %all-gather.5.cloned.1.call-done, bf16[896,2048]{1,0:T(8,128)(2,1)} %param.5), kind=kOutput, calls=%fused_computation.85 | convolution fusion | flops 3758096384 | bytes 11534336 | tf_op jit(solution)/shard_map/dot_general | solution.py:101
  409.2 5.0 reshape_reshape.6
  414.2 3.1 copy.98
  417.3 52.6 %all_to_all.53 = f32[32,8,1,4,896]{4,3,1,2,0:T(4,128)} all-to-all(f32[32,8,1,4,896]{4,3,1,2,0:T(4,128)S(1)} %bitcast.161), channel_id=1, replica_groups=mesh['ctx'=8,'vocab'=32] {'vocab'}, dimensions={0} | all-to-all | bytes 7340032 | tf_op jit(solution)/shard_map/all_to_all | solution.py:56
  469.9 2.7 reduce_sum.29
  472.6 12.3 %all_to_all.54 = bf16[8,1,4,896]{3,2,1,0:T(4,128)(2,1)S(1)} all-to-all(bf16[8,1,4,896]{3,2,1,0:T(4,128)(2,1)S(1)} %bitcast.197), channel_id=1, replica_groups=mesh['ctx'=8,'vocab'=32] {'ctx'}, dimensions={0} | all-to-all | bytes 114688 | tf_op jit(solution)/shard_map/all_to_all | solution.py:111
  484.9 0.6 constant_dynamic-update-slice_fusion.31
  485.5 0.7 constant_dynamic-update-slice_fusion.30
  486.1 0.7 constant_dynamic-update-slice_fusion.29
  486.8 0.7 constant_dynamic-update-slice_fusion.28
  487.4 0.6 constant_dynamic-update-slice_fusion.27
  488.0 0.7 constant_dynamic-update-slice_fusion.26
  488.7 0.7 constant_dynamic-update-slice_fusion.25
  489.3 0.7 constant_dynamic-update-slice_fusion.24
  490.0 0.6 constant_dynamic-update-slice_fusion.23
  490.6 0.7 constant_dynamic-update-slice_fusion.22
  491.2 0.7 constant_dynamic-update-slice_fusion.21
  491.9 0.7 constant_dynamic-update-slice_fusion.20
  492.5 0.6 constant_dynamic-update-slice_fusion.19
  493.1 0.7 constant_dynamic-update-slice_fusion.18
  493.8 0.7 constant_dynamic-update-slice_fusion.17
  494.4 0.7 constant_dynamic-update-slice_fusion.16
  495.1 0.6 constant_dynamic-update-slice_fusion.15
  495.6 0.7 constant_dynamic-update-slice_fusion.14
  496.3 0.7 constant_dynamic-update-slice_fusion.13
  496.9 0.7 constant_dynamic-update-slice_fusion.12
  497.6 0.6 constant_dynamic-update-slice_fusion.11
  498.2 0.7 constant_dynamic-update-slice_fusion.10
  498.8 0.7 constant_dynamic-update-slice_fusion.9
  499.5 0.7 constant_dynamic-update-slice_fusion.8
  500.1 0.6 constant_dynamic-update-slice_fusion.7
  500.7 0.7 constant_dynamic-update-slice_fusion.6
  501.4 0.7 constant_dynamic-update-slice_fusion.5
  502.0 0.7 constant_dynamic-update-slice_fusion.4
  502.7 0.6 constant_dynamic-update-slice_fusion.3
  503.3 0.7 constant_dynamic-update-slice_fusion.2
  503.9 0.7 constant_dynamic-update-slice_fusion.1
  504.6 0.7 constant_dynamic-update-slice_fusion
  505.2 3.9 all-to-all-start.4
  509.1 0.1 sub.71
  509.2 0.6 copy.93
  509.8 6.5 %all-to-all-done.4 = bf16[32,1,1,4,224]{4,3,2,1,0:T(4,128)(2,1)S(1)} async-done(((bf16[32,1,1,4,224]{4,3,2,1,0:T(4,128)(2,1)}), bf16[32,1,1,4,224]{4,3,2,1,0:T(4,128)(2,1)S(1)}, u32[]{:S(2)}, u32[]{:S(2)}) %all-to-all-start.4) | async-done | bytes 57376 | tf_op jit(solution)/shard_map/all_to_all | solution.py:10
  516.3 0.7 reshape_reshape.7
  (43 shorter events, 0.6 us)
Async XLA Ops:
  7.2 143.0 %all-gather.3.cloned.1.call-start = ((), (), s32[]{:S(2)}) async-start(), calls=%async_computation.6 | async-start | bytes 1892352 | tf_op jit(solution)/shard_map/all_gather | solution.py:79
  8.9 316.6 %reduce-scatter.2.cloned.1.call-start = ((), (), s32[]{:S(2)}) async-start(), calls=%async_computation.7 | async-start | bytes 9437184 | tf_op jit(solution)/shard_map/reduce_scatter | solution.py:81
  235.9 0.7 copy-start
  235.9 101.5 %copy-start.1 = (f32[64,2]{0,1:T(2,128)S(1)}, f32[64,2]{0,1:T(2,128)}, u32[]{:S(2)}) copy-start(f32[64,2]{0,1:T(2,128)} %param.7) | copy-start | bytes 1540
  329.1 15.5 %all-to-all-start.1 = ((f32[32,3,128]{2,1,0:T(4,128)}), f32[32,3,128]{2,1,0:T(4,128)S(1)}, u32[]{:S(2)}, u32[]{:S(2)}) async-start(f32[32,3,128]{2,1,0:T(4,128)} %broadcast_in_dim.9), calls=%async_computation.2 | async-start | bytes 131072 | tf_op jit(solution)/shard_map/all_to_all | solution.py:15
  337.4 62.1 %all-gather.5.cloned.1.call-start = ((), (), s32[]{:S(2)}) async-start(), calls=%async_computation.8 | async-start | bytes 4718592 | tf_op jit(solution)/shard_map/all_gather | solution.py:102
  505.2 11.1 %all-to-all-start.4 = ((bf16[32,1,1,4,224]{4,3,2,1,0:T(4,128)(2,1)}), bf16[32,1,1,4,224]{4,3,2,1,0:T(4,128)(2,1)S(1)}, u32[]{:S(2)}, u32[]{:S(2)}) async-start(bf16[32,1,1,4,224]{4,3,2,1,0:T(4,128)(2,1)} %constant_dynamic-update-slice_fusion), calls=%async_computation.5 | async-start | bytes 131072 | tf_op jit(solution)/shard_map/all_to_all | solution.py:10
Sparse Core Ops, SparseCore 0:
  10.3 139.7 all-gather.2
  236.1 89.3 reduce-scatter.1
  347.8 51.7 all-gather.4
